TPU v7x, 128 devices: a whole 4x4x4 slice. The times are simulated.
128 devices in a mesh: grp: 2 (over core), row: 8 (over x_lo, y), col: 8 (over z, x_hi).
Axes of the slice: x: 4 (x_hi: 2, x_lo: 2; x = x_hi * 2 + x_lo), y: 4, z: 4, core: 2. Of those that a mesh axis runs over, the one named last changes fastest.
Arguments:
- conserved: float32 [5, 512, 4096], P(None, 'row', 'col'), may hold values from -1 to 5.5, as said below
- displacement: float32 [2, 512, 4096], P(None, ('row', 'col')), may hold values from -0.3 to 0.3
Outputs:
- group_fields: float32 [2, 5, 512, 4096], P('grp', None, 'row', 'col')
Inputs may be any that keep to these rules, and one draw needn't show every extreme that they name: `conserved`: per cell: density and pressure (0.4 times the energy minus the kinetic energy) lie between 1 and 2, both speeds between -0.5 and 0.5, the tracer fraction between 0 and 1.
All inputs are finite; a program needn't handle non-finite values.
Results may differ from a plain program's by a relative error of at most 0.0003.
Values sent between devices are 32-bit elements; how exact they have to be, the bound alone decides.
No kernel may reach another device: no remote copies, remote signals or barrier semaphores. Data moves between devices by JAX's collectives and lax.ppermute only.
A program may use at most 64 MiB of HBM per device.

v0:
```python
import jax
import jax.numpy as jnp
from jax import lax
from jax.sharding import PartitionSpec as P

STEPS = 2
SWEEPS = 4
HEAT_RATIO = 1.4
TIME_STEP = 0.08
GRADIENT_GAIN = 8.0
MONITOR_GAIN = 0.2
RELAXATION = 0.5


def partner(block, axis, apart):
    count = lax.axis_size(axis)
    route = []
    for low in range(count):
        high = low | 1 << apart
        if high != low and high < count:
            route += [(low, high), (high, low)]
    return lax.ppermute(block, axis, route)


def with_halo(cells, sides, width):
    for axis, dim in sides:
        count = lax.axis_size(axis)
        head = lax.slice_in_dim(cells, 0, width, axis=dim)
        tail = lax.slice_in_dim(cells, cells.shape[dim] - width, cells.shape[dim], axis=dim)
        cells = jnp.concatenate(
            [
                lax.ppermute(tail, axis, [(i, (i + 1) % count) for i in range(count)]),
                cells,
                lax.ppermute(head, axis, [((i + 1) % count, i) for i in range(count)]),
            ],
            axis=dim,
        )
    return cells


def minmod(lower_diff, upper_diff):
    smaller = jnp.where(jnp.abs(lower_diff) < jnp.abs(upper_diff), lower_diff, upper_diff)
    return jnp.where(lower_diff * upper_diff > 0.0, smaller, 0.0)


def primitives(fields):
    density = fields[0]
    speed_x = fields[1] / density
    speed_y = fields[2] / density
    pressure = (HEAT_RATIO - 1.0) * (fields[3] - 0.5 * (fields[1] * speed_x + fields[2] * speed_y))
    tracer = fields[4] / density
    return jnp.stack([density, speed_x, speed_y, pressure, tracer])


def normal_flux(states, normal_x, normal_y):
    density, speed_x, speed_y, pressure, tracer = (
        states[0],
        states[1],
        states[2],
        states[3],
        states[4],
    )
    normal_speed = speed_x * normal_x + speed_y * normal_y
    energy = pressure / (HEAT_RATIO - 1.0) + 0.5 * density * (speed_x * speed_x + speed_y * speed_y)
    conserved = jnp.stack([density, density * speed_x, density * speed_y, energy, density * tracer])
    flux_terms = jnp.stack(
        [
            density * normal_speed,
            density * speed_x * normal_speed + pressure * normal_x,
            density * speed_y * normal_speed + pressure * normal_y,
            (energy + pressure) * normal_speed,
            density * tracer * normal_speed,
        ]
    )
    wave_speed = jnp.abs(normal_speed) + jnp.sqrt(HEAT_RATIO * pressure / density) * jnp.sqrt(
        normal_x * normal_x + normal_y * normal_y
    )
    return (conserved, flux_terms, wave_speed)


def rusanov(left_state, right_state, normal_x, normal_y):
    cons_left, flux_left, wave_left = normal_flux(left_state, normal_x, normal_y)
    cons_right, flux_right, wave_right = normal_flux(right_state, normal_x, normal_y)
    wave_speed = jnp.maximum(wave_left, wave_right)
    return 0.5 * (flux_left + flux_right) - 0.5 * wave_speed * (cons_right - cons_left)


def face_states(primitive, along_axis):
    extent = primitive.shape[along_axis]
    differences = lax.slice_in_dim(primitive, 1, extent, axis=along_axis) - lax.slice_in_dim(
        primitive, 0, extent - 1, axis=along_axis
    )
    slopes = minmod(
        lax.slice_in_dim(differences, 0, extent - 2, axis=along_axis),
        lax.slice_in_dim(differences, 1, extent - 1, axis=along_axis),
    )
    left_state = lax.slice_in_dim(
        primitive, 1, extent - 2, axis=along_axis
    ) + 0.5 * lax.slice_in_dim(slopes, 0, extent - 3, axis=along_axis)
    right_state = lax.slice_in_dim(
        primitive, 2, extent - 1, axis=along_axis
    ) - 0.5 * lax.slice_in_dim(slopes, 1, extent - 2, axis=along_axis)
    return (left_state, right_state)


def advance(extended):
    primitive = primitives(extended[:5])
    shift_x = extended[5]
    shift_y = extended[6]
    slope_x_col = 1.0 + 0.5 * (shift_x[1:-1, 2:] - shift_x[1:-1, :-2])
    slope_x_row = 0.5 * (shift_x[2:, 1:-1] - shift_x[:-2, 1:-1])
    slope_y_col = 0.5 * (shift_y[1:-1, 2:] - shift_y[1:-1, :-2])
    slope_y_row = 1.0 + 0.5 * (shift_y[2:, 1:-1] - shift_y[:-2, 1:-1])
    normal_x = 0.5 * (slope_y_row[1:-1, :-1] + slope_y_row[1:-1, 1:])
    normal_y = -0.5 * (slope_x_row[1:-1, :-1] + slope_x_row[1:-1, 1:])
    left_state, right_state = face_states(primitive[:, 2:-2, :], 2)
    col_flux = rusanov(left_state, right_state, normal_x, normal_y)
    normal_x = -0.5 * (slope_y_col[:-1, 1:-1] + slope_y_col[1:, 1:-1])
    normal_y = 0.5 * (slope_x_col[:-1, 1:-1] + slope_x_col[1:, 1:-1])
    left_state, right_state = face_states(primitive[:, :, 2:-2], 1)
    row_flux = rusanov(left_state, right_state, normal_x, normal_y)
    jacobian = (
        slope_x_col[1:-1, 1:-1] * slope_y_row[1:-1, 1:-1]
        - slope_x_row[1:-1, 1:-1] * slope_y_col[1:-1, 1:-1]
    )
    change = col_flux[:, :, 1:] - col_flux[:, :, :-1] + (row_flux[:, 1:, :] - row_flux[:, :-1, :])
    return extended[:5, 2:-2, 2:-2] - TIME_STEP / jacobian * change


def monitor(density, pressure):
    density_col = 0.5 * (density[1:-1, 2:] - density[1:-1, :-2])
    density_row = 0.5 * (density[2:, 1:-1] - density[:-2, 1:-1])
    pressure_col = 0.5 * (pressure[1:-1, 2:] - pressure[1:-1, :-2])
    pressure_row = 0.5 * (pressure[2:, 1:-1] - pressure[:-2, 1:-1])
    strength = GRADIENT_GAIN * (
        density_col * density_col
        + density_row * density_row
        + pressure_col * pressure_col
        + pressure_row * pressure_row
    )
    return 1.0 + MONITOR_GAIN * strength / (1.0 + strength)


def jacobi(shifts, weight):
    center = weight[1:-1, 1:-1]
    east_face = 0.5 * (center + weight[1:-1, 2:])
    west_face = 0.5 * (center + weight[1:-1, :-2])
    north_face = 0.5 * (center + weight[2:, 1:-1])
    south_face = 0.5 * (center + weight[:-2, 1:-1])
    face_total = east_face + west_face + north_face + south_face
    middle = shifts[:, 1:-1, 1:-1]
    beside_all = (
        east_face * shifts[:, 1:-1, 2:]
        + west_face * shifts[:, 1:-1, :-2]
        + north_face * shifts[:, 2:, 1:-1]
        + south_face * shifts[:, :-2, 1:-1]
    )
    source = jnp.stack([east_face - west_face, north_face - south_face])
    target = (beside_all + source) / face_total
    return middle + RELAXATION * (target - middle)


def pair_of(fields):
    primitive = primitives(fields)
    return jnp.stack([primitive[0], primitive[3]])


def on_device(conserved, displacement):
    on_mesh = lax.axis_index("grp") == 1
    column_count = lax.axis_size("col")
    block_rows = conserved.shape[1]
    block_cols = conserved.shape[2]
    slab_rows = displacement.shape[1]

    def to_pieces_block(values):
        return values.reshape(values.shape[0], column_count, slab_rows, block_cols)

    def to_pieces_slab(values):
        return values.reshape(values.shape[0], slab_rows, column_count, block_cols).transpose(
            0, 2, 1, 3
        )

    def from_pieces_block(values):
        return values.reshape(values.shape[0], block_rows, block_cols)

    def from_pieces_slab(values):
        return values.transpose(0, 2, 1, 3).reshape(
            values.shape[0], slab_rows, column_count * block_cols
        )

    def regroup(values):
        return lax.all_to_all(values, "col", split_axis=1, concat_axis=1, tiled=True)

    def only_mesh(worker, fallback, operands):
        return lax.cond(on_mesh, lambda packed: worker(*packed), lambda packed: fallback, operands)

    def slab_extend(values, margin):
        extended = with_halo(values, ((("row", "col"), 1),), margin)
        return jnp.concatenate(
            [extended[:, :, -margin:], extended, extended[:, :, :margin]], axis=2
        )

    pairs_block = pair_of(conserved)
    arrived = regroup(
        jnp.where(on_mesh, to_pieces_block(pairs_block), to_pieces_slab(displacement))
    )
    shifts_block = from_pieces_block(arrived)
    pairs_mesh = from_pieces_slab(arrived)
    shifts_mesh = displacement
    current = conserved
    previous = shifts_mesh
    weight = jnp.zeros(shifts_mesh.shape[1:], jnp.float32)
    for step_index in range(STEPS):
        physics_extended = with_halo(
            jnp.concatenate([current, shifts_block]), (("row", 1), ("col", 2)), 2
        )
        only_fallback = current
        new_state = lax.cond(
            on_mesh,
            lambda packed: only_fallback,
            lambda packed: advance(*packed),
            (physics_extended,),
        )
        shifts = shifts_mesh
        mesh_extended = slab_extend(jnp.concatenate([pairs_mesh, shifts]), 2)
        blank = jnp.zeros((mesh_extended.shape[1] - 2, mesh_extended.shape[2] - 2), jnp.float32)
        weight_cycle = only_mesh(monitor, blank, (mesh_extended[0], mesh_extended[1]))
        rim_shifts = mesh_extended[2:4, 1:-1, 1:-1]
        for sweep_index in range(SWEEPS):
            if sweep_index > 0:
                rim_shifts = slab_extend(shifts, 1)
            shifts = only_mesh(jacobi, shifts, (rim_shifts, weight_cycle))
        mesh_weight = weight_cycle[1:-1, 1:-1]
        weight = mesh_weight
        if step_index + 1 < STEPS:
            new_pairs = pair_of(new_state)
            outgoing = jnp.where(on_mesh, to_pieces_slab(shifts), to_pieces_block(new_pairs))
            arrived = partner(regroup(outgoing), "grp", 0)
            shifts_block = from_pieces_block(arrived)
            pairs_mesh = from_pieces_slab(arrived)
        previous = shifts_mesh
        shifts_mesh = shifts
        current = new_state
    mesh_fields = jnp.stack(
        [
            shifts_mesh[0],
            shifts_mesh[1],
            (shifts_mesh[0] - previous[0]) / TIME_STEP,
            (shifts_mesh[1] - previous[1]) / TIME_STEP,
            weight,
        ]
    )
    mesh_fields = from_pieces_block(regroup(to_pieces_slab(mesh_fields)))
    return jnp.where(on_mesh, mesh_fields, current)[None]


def solution(mesh):
    placed = (P(None, "row", "col"), P(None, ("row", "col"), None))
    return jax.shard_map(
        on_device,
        mesh=mesh,
        in_specs=placed,
        out_specs=P("grp", None, "row", "col"),
        check_vma=False,
    )
```

profile of v0, /device:TPU:0, one launch (start us, length us, event | category | flops | bytes accessed | tf_op | source)
XLA Modules:
  0.0 186.9 jit_solution(14474896401639339898)
XLA Ops:
  0.0 0.9 copy.135
  1.0 1.1 slice_bitcast_fusion.9
  2.2 16.5 %all_to_all.15 = f32[2,8,8,512]{3,2,0,1:T(8,128)S(1)} all-to-all(f32[2,8,8,512]{3,2,0,1:T(8,128)S(1)} %copy.13), channel_id=1, replica_groups=mesh['grp'=2,'row'=8,'col'=8] {'col'}, dimensions={1} | all-to-all | bytes 524288 | tf_op jit(solution)/shard_map/all_to_all | solution.py:192
  18.8 3.7 %collective-permute-start.1 = (f32[4,2,4096]{2,1,0:T(2,128)S(1)}, f32[4,2,4096]{2,1,0:T(2,128)S(1)}, u32[]{:S(2)}, u32[]{:S(2)}) collective-permute-start(f32[4,2,4096]{2,1,0:T(2,128)S(1)} %get-tuple-element.352), channel_id=1, source_target_pairs={{1,0},{2,1},{3,2},{4,3},{5,4},{6,5},{7,6},{8,7},{9,8},{10,9},{11,1... | collective-permute-start | bytes 393224 | tf_op jit(solution)/shard_map/ppermute | solution.py:34
  22.6 3.0 %collective-permute-start.9 = (f32[7,2,512]{2,1,0:T(2,128)S(1)}, f32[7,2,512]{2,1,0:T(2,128)S(1)}, u32[]{:S(2)}, u32[]{:S(2)}) collective-permute-start(f32[7,2,512]{2,1,0:T(2,128)S(1)} %get-tuple-element.330), channel_id=1, source_target_pairs={{8,0},{16,8},{24,16},{32,24},{40,32},{48,40},{56,48},{0,56},{9,1},... | collective-permute-start | bytes 86024 | tf_op jit(solution)/shard_map/ppermute | solution.py:34
  25.6 0.9 collective-permute-done.1
  26.5 6.7 %collective-permute-done = f32[4,2,4096]{2,1,0:T(2,128)S(1)} collective-permute-done((f32[4,2,4096]{2,1,0:T(2,128)S(1)}, f32[4,2,4096]{2,1,0:T(2,128)S(1)}, u32[]{:S(2)}, u32[]{:S(2)}) %collective-permute-start) | collective-permute-done | bytes 131104 | tf_op jit(solution)/shard_map/ppermute | solution.py:32
  33.5 0.9 copy-done.1
  34.4 1.6 concatenate.79
  36.1 1.3 collective-permute-start.3
  37.4 2.3 %collective-permute-start.2 = (f32[2,1,4096]{2,1,0:T(1,128)S(1)}, f32[2,1,4096]{2,1,0:T(1,128)S(1)}, u32[]{:S(2)}, u32[]{:S(2)}) collective-permute-start(f32[2,1,4096]{2,1,0:T(1,128)S(1)} %get-tuple-element.363), channel_id=1, source_target_pairs={{0,1},{1,2},{2,3},{3,4},{4,5},{5,6},{6,7},{7,8},{8,9},{9,10},{10,1... | collective-permute-start | bytes 98312 | tf_op jit(solution)/shard_map/ppermute | solution.py:32
  39.9 1.4 collective-permute-start.11
  41.3 2.2 %collective-permute-start.10 = (f32[7,68,2]{2,1,0:T(8,128)S(1)}, f32[7,68,2]{2,1,0:T(8,128)}, u32[]{:S(2)}, u32[]{:S(2)}) collective-permute-start(f32[7,68,2]{2,1,0:T(8,128)S(1)} %get-tuple-element.325), channel_id=1, source_target_pairs={{0,1},{1,2},{2,3},{3,4},{4,5},{5,6},{6,7},{7,0},{8,9},{9,10},{10,1... | collective-permute-start | bytes 11432 | tf_op jit(solution)/shard_map/ppermute | solution.py:32
  43.5 7.2 %collective-permute-done.3 = f32[2,1,4096]{2,1,0:T(1,128)S(1)} collective-permute-done((f32[2,1,4096]{2,1,0:T(1,128)S(1)}, f32[2,1,4096]{2,1,0:T(1,128)S(1)}, u32[]{:S(2)}, u32[]{:S(2)}) %collective-permute-start.3) | collective-permute-done | bytes 32800 | tf_op jit(solution)/shard_map/ppermute | solution.py:34
  50.7 3.7 %collective-permute-done.2 = f32[2,1,4096]{2,1,0:T(1,128)S(1)} collective-permute-done((f32[2,1,4096]{2,1,0:T(1,128)S(1)}, f32[2,1,4096]{2,1,0:T(1,128)S(1)}, u32[]{:S(2)}, u32[]{:S(2)}) %collective-permute-start.2) | collective-permute-done | bytes 32800 | tf_op jit(solution)/shard_map/ppermute | solution.py:32
  54.9 4.3 %collective-permute-start.5 = (f32[2,1,4096]{2,1,0:T(1,128)S(1)}, f32[2,1,4096]{2,1,0:T(1,128)S(1)}, u32[]{:S(2)}, u32[]{:S(2)}) collective-permute-start(f32[2,1,4096]{2,1,0:T(1,128)S(1)} %get-tuple-element.362), channel_id=1, source_target_pairs={{1,0},{2,1},{3,2},{4,3},{5,4},{6,5},{7,6},{8,7},{9,8},{10,9},{11,1... | collective-permute-start | bytes 98312 | tf_op jit(solution)/shard_map/ppermute | solution.py:34
  59.2 1.7 pad_maximum_fusion
  60.9 6.8 %conditional.17 = (f32[5,64,512]{2,1,0:T(8,128)S(1)}) conditional(s32[]{:T(128)} %convert_element_type.2, (f32[7,68,516]{2,1,0:T(8,128)S(1)}, f32[5,64,512]{2,1,0:T(8,128)S(1)}) %tuple.239, f32[5,64,512]{2,1,0:T(8,128)S(1)} %copy-done), branch_computations={%region_10.11_spmd, %region_11.12_spmd} | conditional | flops 12940432 | bytes 60802312 | solution.py:218
  69.0 6.7 %collective-permute-start.7 = (f32[2,1,4096]{2,1,0:T(1,128)S(1)}, f32[2,1,4096]{2,1,0:T(1,128)S(1)}, u32[]{:S(2)}, u32[]{:S(2)}) collective-permute-start(f32[2,1,4096]{2,1,0:T(1,128)S(1)} %get-tuple-element.360), channel_id=1, source_target_pairs={{1,0},{2,1},{3,2},{4,3},{5,4},{6,5},{7,6},{8,7},{9,8},{10,9},{11,1... | collective-permute-start | bytes 98312 | tf_op jit(solution)/shard_map/ppermute | solution.py:34
  75.7 1.5 collective-permute-done.7
  77.3 8.1 %collective-permute-done.6 = f32[2,1,4096]{2,1,0:T(1,128)S(1)} collective-permute-done((f32[2,1,4096]{2,1,0:T(1,128)S(1)}, f32[2,1,4096]{2,1,0:T(1,128)S(1)}, u32[]{:S(2)}, u32[]{:S(2)}) %collective-permute-start.6) | collective-permute-done | bytes 32800 | tf_op jit(solution)/shard_map/ppermute | solution.py:32
  85.9 11.2 %all_to_all.16 = f32[2,8,8,512]{3,2,0,1:T(8,128)S(1)} all-to-all(f32[2,8,8,512]{3,2,0,1:T(8,128)S(1)} %copy.17), channel_id=1, replica_groups=mesh['grp'=2,'row'=8,'col'=8] {'col'}, dimensions={1} | all-to-all | bytes 524288 | tf_op jit(solution)/shard_map/all_to_all | solution.py:192
  97.2 1.5 collective-permute-done.12
  98.8 1.2 collective-permute-start.14
  100.1 2.4 %collective-permute-start.13 = (f32[4,2,4096]{2,1,0:T(2,128)S(1)}, f32[4,2,4096]{2,1,0:T(2,128)S(1)}, u32[]{:S(2)}, u32[]{:S(2)}) collective-permute-start(f32[4,2,4096]{2,1,0:T(2,128)S(1)} %get-tuple-element.343), channel_id=1, source_target_pairs={{0,1},{1,2},{2,3},{3,4},{4,5},{5,6},{6,7},{7,8},{8,9},{9,10},{10,1... | collective-permute-start | bytes 393224 | tf_op jit(solution)/shard_map/ppermute | solution.py:32
  102.4 4.3 %collective-permute-done.14 = f32[4,2,4096]{2,1,0:T(2,128)S(1)} collective-permute-done((f32[4,2,4096]{2,1,0:T(2,128)S(1)}, f32[4,2,4096]{2,1,0:T(2,128)S(1)}, u32[]{:S(2)}, u32[]{:S(2)}) %collective-permute-start.14) | collective-permute-done | bytes 131104 | tf_op jit(solution)/shard_map/ppermute | solution.py:34
  106.8 4.3 %collective-permute-done.13 = f32[4,2,4096]{2,1,0:T(2,128)S(1)} collective-permute-done((f32[4,2,4096]{2,1,0:T(2,128)S(1)}, f32[4,2,4096]{2,1,0:T(2,128)S(1)}, u32[]{:S(2)}, u32[]{:S(2)}) %collective-permute-start.13) | collective-permute-done | bytes 131104 | tf_op jit(solution)/shard_map/ppermute | solution.py:32
  111.4 0.9 copy-done.2
  112.3 1.7 concatenate.91
  115.2 3.5 %collective-permute-start.15 = (f32[2,1,4096]{2,1,0:T(1,128)S(1)}, f32[2,1,4096]{2,1,0:T(1,128)S(1)}, u32[]{:S(2)}, u32[]{:S(2)}) collective-permute-start(f32[2,1,4096]{2,1,0:T(1,128)S(1)} %get-tuple-element.357), channel_id=1, source_target_pairs={{0,1},{1,2},{2,3},{3,4},{4,5},{5,6},{6,7},{7,8},{8,9},{9,10},{10,1... | collective-permute-start | bytes 98312 | tf_op jit(solution)/shard_map/ppermute | solution.py:32
  118.7 1.9 %collective-permute-done.16 = f32[2,1,4096]{2,1,0:T(1,128)S(1)} collective-permute-done((f32[2,1,4096]{2,1,0:T(1,128)S(1)}, f32[2,1,4096]{2,1,0:T(1,128)S(1)}, u32[]{:S(2)}, u32[]{:S(2)}) %collective-permute-start.16) | collective-permute-done | bytes 32800 | tf_op jit(solution)/shard_map/ppermute | solution.py:34
  120.6 4.0 %collective-permute-done.15 = f32[2,1,4096]{2,1,0:T(1,128)S(1)} collective-permute-done((f32[2,1,4096]{2,1,0:T(1,128)S(1)}, f32[2,1,4096]{2,1,0:T(1,128)S(1)}, u32[]{:S(2)}, u32[]{:S(2)}) %collective-permute-start.15) | collective-permute-done | bytes 32800 | tf_op jit(solution)/shard_map/ppermute | solution.py:32
  125.2 3.5 %collective-permute-start.17 = (f32[2,1,4096]{2,1,0:T(1,128)S(1)}, f32[2,1,4096]{2,1,0:T(1,128)S(1)}, u32[]{:S(2)}, u32[]{:S(2)}) collective-permute-start(f32[2,1,4096]{2,1,0:T(1,128)S(1)} %get-tuple-element.355), channel_id=1, source_target_pairs={{0,1},{1,2},{2,3},{3,4},{4,5},{5,6},{6,7},{7,8},{8,9},{9,10},{10,1... | collective-permute-start | bytes 98312 | tf_op jit(solution)/shard_map/ppermute | solution.py:32
  128.7 1.9 %collective-permute-done.18 = f32[2,1,4096]{2,1,0:T(1,128)S(1)} collective-permute-done((f32[2,1,4096]{2,1,0:T(1,128)S(1)}, f32[2,1,4096]{2,1,0:T(1,128)S(1)}, u32[]{:S(2)}, u32[]{:S(2)}) %collective-permute-start.18) | collective-permute-done | bytes 32800 | tf_op jit(solution)/shard_map/ppermute | solution.py:34
  130.6 4.0 %collective-permute-done.17 = f32[2,1,4096]{2,1,0:T(1,128)S(1)} collective-permute-done((f32[2,1,4096]{2,1,0:T(1,128)S(1)}, f32[2,1,4096]{2,1,0:T(1,128)S(1)}, u32[]{:S(2)}, u32[]{:S(2)}) %collective-permute-start.17) | collective-permute-done | bytes 32800 | tf_op jit(solution)/shard_map/ppermute | solution.py:32
  135.3 3.5 %collective-permute-start.19 = (f32[2,1,4096]{2,1,0:T(1,128)S(1)}, f32[2,1,4096]{2,1,0:T(1,128)S(1)}, u32[]{:S(2)}, u32[]{:S(2)}) collective-permute-start(f32[2,1,4096]{2,1,0:T(1,128)S(1)} %get-tuple-element.353), channel_id=1, source_target_pairs={{0,1},{1,2},{2,3},{3,4},{4,5},{5,6},{6,7},{7,8},{8,9},{9,10},{10,1... | collective-permute-start | bytes 98312 | tf_op jit(solution)/shard_map/ppermute | solution.py:32
  138.8 1.9 %collective-permute-done.20 = f32[2,1,4096]{2,1,0:T(1,128)S(1)} collective-permute-done((f32[2,1,4096]{2,1,0:T(1,128)S(1)}, f32[2,1,4096]{2,1,0:T(1,128)S(1)}, u32[]{:S(2)}, u32[]{:S(2)}) %collective-permute-start.20) | collective-permute-done | bytes 32800 | tf_op jit(solution)/shard_map/ppermute | solution.py:34
  140.7 7.0 %collective-permute-done.19 = f32[2,1,4096]{2,1,0:T(1,128)S(1)} collective-permute-done((f32[2,1,4096]{2,1,0:T(1,128)S(1)}, f32[2,1,4096]{2,1,0:T(1,128)S(1)}, u32[]{:S(2)}, u32[]{:S(2)}) %collective-permute-start.19) | collective-permute-done | bytes 32800 | tf_op jit(solution)/shard_map/ppermute | solution.py:32
  148.7 1.2 copy.20
  149.9 3.5 %all-to-all-start.2 = ((f32[5,8,8,512]{3,2,0,1:T(8,128)}), f32[5,8,8,512]{3,2,0,1:T(8,128)S(1)}, u32[]{:S(2)}, u32[]{:S(2)}) async-start(f32[5,8,8,512]{3,2,0,1:T(8,128)} %copy.20), calls=%async_computation.2 | async-start | bytes 1310720 | tf_op jit(solution)/shard_map/all_to_all | solution.py:192
  153.6 2.0 %collective-permute-start.21 = (f32[7,2,512]{2,1,0:T(2,128)S(1)}, f32[7,2,512]{2,1,0:T(2,128)S(1)}, u32[]{:S(2)}, u32[]{:S(2)}) collective-permute-start(f32[7,2,512]{2,1,0:T(2,128)S(1)} %get-tuple-element.327), channel_id=1, source_target_pairs={{0,8},{8,16},{16,24},{24,32},{32,40},{40,48},{48,56},{56,0},{1,9},... | collective-permute-start | bytes 86024 | tf_op jit(solution)/shard_map/ppermute | solution.py:32
  155.6 2.9 %collective-permute-done.22 = f32[7,2,512]{2,1,0:T(2,128)S(1)} collective-permute-done((f32[7,2,512]{2,1,0:T(2,128)S(1)}, f32[7,2,512]{2,1,0:T(2,128)S(1)}, u32[]{:S(2)}, u32[]{:S(2)}) %collective-permute-start.22) | collective-permute-done | bytes 28704 | tf_op jit(solution)/shard_map/ppermute | solution.py:34
  158.5 1.4 collective-permute-done.21
  160.1 5.6 %collective-permute-start.24 = (f32[7,68,2]{2,1,0:T(8,128)S(1)}, f32[7,68,2]{2,1,0:T(8,128)S(1)}, u32[]{:S(2)}, u32[]{:S(2)}) collective-permute-start(f32[7,68,2]{2,1,0:T(8,128)S(1)} %get-tuple-element.324), channel_id=1, source_target_pairs={{1,0},{2,1},{3,2},{4,3},{5,4},{6,5},{7,6},{0,7},{9,8},{10,9},{11,1... | collective-permute-start | bytes 11432 | tf_op jit(solution)/shard_map/ppermute | solution.py:34
  165.7 4.3 %collective-permute-done.24 = f32[7,68,2]{2,1,0:T(8,128)S(1)} collective-permute-done((f32[7,68,2]{2,1,0:T(8,128)S(1)}, f32[7,68,2]{2,1,0:T(8,128)S(1)}, u32[]{:S(2)}, u32[]{:S(2)}) %collective-permute-start.24) | collective-permute-done | bytes 3840 | tf_op jit(solution)/shard_map/ppermute | solution.py:34
  170.0 8.4 %collective-permute-done.23 = f32[7,68,2]{2,1,0:T(8,128)S(1)} collective-permute-done((f32[7,68,2]{2,1,0:T(8,128)S(1)}, f32[7,68,2]{2,1,0:T(8,128)S(1)}, u32[]{:S(2)}, u32[]{:S(2)}) %collective-permute-start.23) | collective-permute-done | bytes 3840 | tf_op jit(solution)/shard_map/ppermute | solution.py:32
  179.0 6.9 %conditional.23 = (f32[5,64,512]{2,1,0:T(8,128)S(1)}) conditional(s32[]{:T(128)} %convert_element_type.2, (f32[7,68,516]{2,1,0:T(8,128)S(1)}, f32[5,64,512]{2,1,0:T(8,128)S(1)}) %tuple.90, f32[5,64,512]{2,1,0:T(8,128)S(1)} %get-tuple-element.376), branch_computations={%region_22.23_spmd, %region_23.24_spmd} | conditional | flops 12940432 | bytes 60802312 | solution.py:218
  185.9 0.9 fusion.218
  (176 shorter events, 21.2 us)
Async XLA Ops:
  18.6 3.9 %copy-start = (f32[5,64,512]{2,1,0:T(8,128)S(1)}, f32[5,64,512]{2,1,0:T(8,128)}, u32[]{:S(2)}) copy-start(f32[5,64,512]{2,1,0:T(8,128)} %param.26) | copy-start | bytes 1966084
  18.8 7.7 %collective-permute-start.1 = (f32[4,2,4096]{2,1,0:T(2,128)S(1)}, f32[4,2,4096]{2,1,0:T(2,128)S(1)}, u32[]{:S(2)}, u32[]{:S(2)}) collective-permute-start(f32[4,2,4096]{2,1,0:T(2,128)S(1)} %get-tuple-element.352), channel_id=1, source_target_pairs={{1,0},{2,1},{3,2},{4,3},{5,4},{6,5},{7,6},{8,7},{9,8},{10,9},{11,1... | collective-permute-start | bytes 393224 | tf_op jit(solution)/shard_map/ppermute | solution.py:34
  22.5 10.7 %collective-permute-start = (f32[4,2,4096]{2,1,0:T(2,128)S(1)}, f32[4,2,4096]{2,1,0:T(2,128)S(1)}, u32[]{:S(2)}, u32[]{:S(2)}) collective-permute-start(f32[4,2,4096]{2,1,0:T(2,128)S(1)} %get-tuple-element.351), channel_id=1, source_target_pairs={{0,1},{1,2},{2,3},{3,4},{4,5},{5,6},{6,7},{7,8},{8,9},{9,10},{10,1... | collective-permute-start | bytes 393224 | tf_op jit(solution)/shard_map/ppermute | solution.py:32
  22.6 17.1 %collective-permute-start.9 = (f32[7,2,512]{2,1,0:T(2,128)S(1)}, f32[7,2,512]{2,1,0:T(2,128)S(1)}, u32[]{:S(2)}, u32[]{:S(2)}) collective-permute-start(f32[7,2,512]{2,1,0:T(2,128)S(1)} %get-tuple-element.330), channel_id=1, source_target_pairs={{8,0},{16,8},{24,16},{32,24},{40,32},{48,40},{56,48},{0,56},{9,1},... | collective-permute-start | bytes 86024 | tf_op jit(solution)/shard_map/ppermute | solution.py:34
  25.6 14.2 %collective-permute-start.8 = (f32[7,2,512]{2,1,0:T(2,128)S(1)}, f32[7,2,512]{2,1,0:T(2,128)S(1)}, u32[]{:S(2)}, u32[]{:S(2)}) collective-permute-start(f32[7,2,512]{2,1,0:T(2,128)S(1)} %get-tuple-element.329), channel_id=1, source_target_pairs={{0,8},{8,16},{16,24},{24,32},{32,40},{40,48},{48,56},{56,0},{1,9},... | collective-permute-start | bytes 86024 | tf_op jit(solution)/shard_map/ppermute | solution.py:32
  33.4 1.0 copy-start.1
  36.1 14.6 %collective-permute-start.3 = (f32[2,1,4096]{2,1,0:T(1,128)S(1)}, f32[2,1,4096]{2,1,0:T(1,128)S(1)}, u32[]{:S(2)}, u32[]{:S(2)}) collective-permute-start(f32[2,1,4096]{2,1,0:T(1,128)S(1)} %get-tuple-element.364), channel_id=1, source_target_pairs={{1,0},{2,1},{3,2},{4,3},{5,4},{6,5},{7,6},{8,7},{9,8},{10,9},{11,1... | collective-permute-start | bytes 98312 | tf_op jit(solution)/shard_map/ppermute | solution.py:34
  37.4 17.0 %collective-permute-start.2 = (f32[2,1,4096]{2,1,0:T(1,128)S(1)}, f32[2,1,4096]{2,1,0:T(1,128)S(1)}, u32[]{:S(2)}, u32[]{:S(2)}) collective-permute-start(f32[2,1,4096]{2,1,0:T(1,128)S(1)} %get-tuple-element.363), channel_id=1, source_target_pairs={{0,1},{1,2},{2,3},{3,4},{4,5},{5,6},{6,7},{7,8},{8,9},{9,10},{10,1... | collective-permute-start | bytes 98312 | tf_op jit(solution)/shard_map/ppermute | solution.py:32
  39.9 19.3 %collective-permute-start.11 = (f32[7,68,2]{2,1,0:T(8,128)S(1)}, f32[7,68,2]{2,1,0:T(8,128)}, u32[]{:S(2)}, u32[]{:S(2)}) collective-permute-start(f32[7,68,2]{2,1,0:T(8,128)S(1)} %get-tuple-element.326), channel_id=1, source_target_pairs={{1,0},{2,1},{3,2},{4,3},{5,4},{6,5},{7,6},{0,7},{9,8},{10,9},{11,1... | collective-permute-start | bytes 11432 | tf_op jit(solution)/shard_map/ppermute | solution.py:34
  41.3 17.9 %collective-permute-start.10 = (f32[7,68,2]{2,1,0:T(8,128)S(1)}, f32[7,68,2]{2,1,0:T(8,128)}, u32[]{:S(2)}, u32[]{:S(2)}) collective-permute-start(f32[7,68,2]{2,1,0:T(8,128)S(1)} %get-tuple-element.325), channel_id=1, source_target_pairs={{0,1},{1,2},{2,3},{3,4},{4,5},{5,6},{6,7},{7,0},{8,9},{9,10},{10,1... | collective-permute-start | bytes 11432 | tf_op jit(solution)/shard_map/ppermute | solution.py:32
  54.9 12.7 %collective-permute-start.5 = (f32[2,1,4096]{2,1,0:T(1,128)S(1)}, f32[2,1,4096]{2,1,0:T(1,128)S(1)}, u32[]{:S(2)}, u32[]{:S(2)}) collective-permute-start(f32[2,1,4096]{2,1,0:T(1,128)S(1)} %get-tuple-element.362), channel_id=1, source_target_pairs={{1,0},{2,1},{3,2},{4,3},{5,4},{6,5},{7,6},{8,7},{9,8},{10,9},{11,1... | collective-permute-start | bytes 98312 | tf_op jit(solution)/shard_map/ppermute | solution.py:34
  59.2 9.3 %collective-permute-start.4 = (f32[2,1,4096]{2,1,0:T(1,128)S(1)}, f32[2,1,4096]{2,1,0:T(1,128)S(1)}, u32[]{:S(2)}, u32[]{:S(2)}) collective-permute-start(f32[2,1,4096]{2,1,0:T(1,128)S(1)} %get-tuple-element.361), channel_id=1, source_target_pairs={{0,1},{1,2},{2,3},{3,4},{4,5},{5,6},{6,7},{7,8},{8,9},{9,10},{10,1... | collective-permute-start | bytes 98312 | tf_op jit(solution)/shard_map/ppermute | solution.py:32
  69.0 8.3 %collective-permute-start.7 = (f32[2,1,4096]{2,1,0:T(1,128)S(1)}, f32[2,1,4096]{2,1,0:T(1,128)S(1)}, u32[]{:S(2)}, u32[]{:S(2)}) collective-permute-start(f32[2,1,4096]{2,1,0:T(1,128)S(1)} %get-tuple-element.360), channel_id=1, source_target_pairs={{1,0},{2,1},{3,2},{4,3},{5,4},{6,5},{7,6},{8,7},{9,8},{10,9},{11,1... | collective-permute-start | bytes 98312 | tf_op jit(solution)/shard_map/ppermute | solution.py:34
  75.7 9.7 %collective-permute-start.6 = (f32[2,1,4096]{2,1,0:T(1,128)S(1)}, f32[2,1,4096]{2,1,0:T(1,128)S(1)}, u32[]{:S(2)}, u32[]{:S(2)}) collective-permute-start(f32[2,1,4096]{2,1,0:T(1,128)S(1)} %get-tuple-element.359), channel_id=1, source_target_pairs={{0,1},{1,2},{2,3},{3,4},{4,5},{5,6},{6,7},{7,8},{8,9},{9,10},{10,1... | collective-permute-start | bytes 98312 | tf_op jit(solution)/shard_map/ppermute | solution.py:32
  97.1 1.6 collective-permute-start.12
  98.8 7.9 %collective-permute-start.14 = (f32[4,2,4096]{2,1,0:T(2,128)S(1)}, f32[4,2,4096]{2,1,0:T(2,128)S(1)}, u32[]{:S(2)}, u32[]{:S(2)}) collective-permute-start(f32[4,2,4096]{2,1,0:T(2,128)S(1)} %get-tuple-element.344), channel_id=1, source_target_pairs={{1,0},{2,1},{3,2},{4,3},{5,4},{6,5},{7,6},{8,7},{9,8},{10,9},{11,1... | collective-permute-start | bytes 393224 | tf_op jit(solution)/shard_map/ppermute | solution.py:34
  100.1 11.0 %collective-permute-start.13 = (f32[4,2,4096]{2,1,0:T(2,128)S(1)}, f32[4,2,4096]{2,1,0:T(2,128)S(1)}, u32[]{:S(2)}, u32[]{:S(2)}) collective-permute-start(f32[4,2,4096]{2,1,0:T(2,128)S(1)} %get-tuple-element.343), channel_id=1, source_target_pairs={{0,1},{1,2},{2,3},{3,4},{4,5},{5,6},{6,7},{7,8},{8,9},{9,10},{10,1... | collective-permute-start | bytes 393224 | tf_op jit(solution)/shard_map/ppermute | solution.py:32
  111.3 1.0 copy-start.2
  115.1 5.5 %collective-permute-start.16 = (f32[2,1,4096]{2,1,0:T(1,128)S(1)}, f32[2,1,4096]{2,1,0:T(1,128)S(1)}, u32[]{:S(2)}, u32[]{:S(2)}) collective-permute-start(f32[2,1,4096]{2,1,0:T(1,128)S(1)} %get-tuple-element.358), channel_id=1, source_target_pairs={{1,0},{2,1},{3,2},{4,3},{5,4},{6,5},{7,6},{8,7},{9,8},{10,9},{11,1... | collective-permute-start | bytes 98312 | tf_op jit(solution)/shard_map/ppermute | solution.py:34
  115.2 9.4 %collective-permute-start.15 = (f32[2,1,4096]{2,1,0:T(1,128)S(1)}, f32[2,1,4096]{2,1,0:T(1,128)S(1)}, u32[]{:S(2)}, u32[]{:S(2)}) collective-permute-start(f32[2,1,4096]{2,1,0:T(1,128)S(1)} %get-tuple-element.357), channel_id=1, source_target_pairs={{0,1},{1,2},{2,3},{3,4},{4,5},{5,6},{6,7},{7,8},{8,9},{9,10},{10,1... | collective-permute-start | bytes 98312 | tf_op jit(solution)/shard_map/ppermute | solution.py:32
  125.1 5.5 %collective-permute-start.18 = (f32[2,1,4096]{2,1,0:T(1,128)S(1)}, f32[2,1,4096]{2,1,0:T(1,128)S(1)}, u32[]{:S(2)}, u32[]{:S(2)}) collective-permute-start(f32[2,1,4096]{2,1,0:T(1,128)S(1)} %get-tuple-element.356), channel_id=1, source_target_pairs={{1,0},{2,1},{3,2},{4,3},{5,4},{6,5},{7,6},{8,7},{9,8},{10,9},{11,1... | collective-permute-start | bytes 98312 | tf_op jit(solution)/shard_map/ppermute | solution.py:34
  125.2 9.4 %collective-permute-start.17 = (f32[2,1,4096]{2,1,0:T(1,128)S(1)}, f32[2,1,4096]{2,1,0:T(1,128)S(1)}, u32[]{:S(2)}, u32[]{:S(2)}) collective-permute-start(f32[2,1,4096]{2,1,0:T(1,128)S(1)} %get-tuple-element.355), channel_id=1, source_target_pairs={{0,1},{1,2},{2,3},{3,4},{4,5},{5,6},{6,7},{7,8},{8,9},{9,10},{10,1... | collective-permute-start | bytes 98312 | tf_op jit(solution)/shard_map/ppermute | solution.py:32
  135.2 5.5 %collective-permute-start.20 = (f32[2,1,4096]{2,1,0:T(1,128)S(1)}, f32[2,1,4096]{2,1,0:T(1,128)S(1)}, u32[]{:S(2)}, u32[]{:S(2)}) collective-permute-start(f32[2,1,4096]{2,1,0:T(1,128)S(1)} %get-tuple-element.354), channel_id=1, source_target_pairs={{1,0},{2,1},{3,2},{4,3},{5,4},{6,5},{7,6},{8,7},{9,8},{10,9},{11,1... | collective-permute-start | bytes 98312 | tf_op jit(solution)/shard_map/ppermute | solution.py:34
  135.3 12.5 %collective-permute-start.19 = (f32[2,1,4096]{2,1,0:T(1,128)S(1)}, f32[2,1,4096]{2,1,0:T(1,128)S(1)}, u32[]{:S(2)}, u32[]{:S(2)}) collective-permute-start(f32[2,1,4096]{2,1,0:T(1,128)S(1)} %get-tuple-element.353), channel_id=1, source_target_pairs={{0,1},{1,2},{2,3},{3,4},{4,5},{5,6},{6,7},{7,8},{8,9},{9,10},{10,1... | collective-permute-start | bytes 98312 | tf_op jit(solution)/shard_map/ppermute | solution.py:32
  149.9 36.0 %all-to-all-start.2 = ((f32[5,8,8,512]{3,2,0,1:T(8,128)}), f32[5,8,8,512]{3,2,0,1:T(8,128)S(1)}, u32[]{:S(2)}, u32[]{:S(2)}) async-start(f32[5,8,8,512]{3,2,0,1:T(8,128)} %copy.20), calls=%async_computation.2 | async-start | bytes 1310720 | tf_op jit(solution)/shard_map/all_to_all | solution.py:192
  153.5 5.0 %collective-permute-start.22 = (f32[7,2,512]{2,1,0:T(2,128)S(1)}, f32[7,2,512]{2,1,0:T(2,128)S(1)}, u32[]{:S(2)}, u32[]{:S(2)}) collective-permute-start(f32[7,2,512]{2,1,0:T(2,128)S(1)} %get-tuple-element.328), channel_id=1, source_target_pairs={{8,0},{16,8},{24,16},{32,24},{40,32},{48,40},{56,48},{0,56},{9,1},... | collective-permute-start | bytes 86024 | tf_op jit(solution)/shard_map/ppermute | solution.py:34
  153.6 6.4 %collective-permute-start.21 = (f32[7,2,512]{2,1,0:T(2,128)S(1)}, f32[7,2,512]{2,1,0:T(2,128)S(1)}, u32[]{:S(2)}, u32[]{:S(2)}) collective-permute-start(f32[7,2,512]{2,1,0:T(2,128)S(1)} %get-tuple-element.327), channel_id=1, source_target_pairs={{0,8},{8,16},{16,24},{24,32},{32,40},{40,48},{48,56},{56,0},{1,9},... | collective-permute-start | bytes 86024 | tf_op jit(solution)/shard_map/ppermute | solution.py:32
  160.1 9.9 %collective-permute-start.24 = (f32[7,68,2]{2,1,0:T(8,128)S(1)}, f32[7,68,2]{2,1,0:T(8,128)S(1)}, u32[]{:S(2)}, u32[]{:S(2)}) collective-permute-start(f32[7,68,2]{2,1,0:T(8,128)S(1)} %get-tuple-element.324), channel_id=1, source_target_pairs={{1,0},{2,1},{3,2},{4,3},{5,4},{6,5},{7,6},{0,7},{9,8},{10,9},{11,1... | collective-permute-start | bytes 11432 | tf_op jit(solution)/shard_map/ppermute | solution.py:34
  165.7 12.7 %collective-permute-start.23 = (f32[7,68,2]{2,1,0:T(8,128)S(1)}, f32[7,68,2]{2,1,0:T(8,128)S(1)}, u32[]{:S(2)}, u32[]{:S(2)}) collective-permute-start(f32[7,68,2]{2,1,0:T(8,128)S(1)} %get-tuple-element.323), channel_id=1, source_target_pairs={{0,1},{1,2},{2,3},{3,4},{4,5},{5,6},{6,7},{7,0},{8,9},{9,10},{10,1... | collective-permute-start | bytes 11432 | tf_op jit(solution)/shard_map/ppermute | solution.py:32
where the time goes:
time: 187 us
  waiting for transfers between devices  77.1 us (41%)
  starting transfers between devices  50.6 us (27%)
  blocking collectives  27.7 us (15%)
  other arithmetic  18.6 us (10%)
  local copies, waits for them, and re-layouts  11.2 us (6%)
    ppermute x12, waiting for transfers between devices, with_halo(): lax.ppermute(tail, axis, [(i, (i + 1) % count) for i in range(count)])  48.6 us
    all_to_all x2, blocking collectives, regroup(): lax.all_to_all(values, 'col', split_axis=1, concat_axis=1, tiled=True)  27.7 us
    ppermute x12, starting transfers between devices, with_halo(): lax.ppermute(head, axis, [((i + 1) % count, i) for i in range(count)])  27.6 us
    ppermute x12, waiting for transfers between devices, with_halo(): lax.ppermute(head, axis, [((i + 1) % count, i) for i in range(count)])  26.9 us
    ppermute x12, starting transfers between devices, with_halo(): lax.ppermute(tail, axis, [(i, (i + 1) % count) for i in range(count)])  19.4 us
    concatenate x8, local copies, waits for them, and re-layouts, slab_extend(): jnp.concatenate([extended[:, :, -margin:], extended, extended[:, :, :marg...  5.05 us
  transfers between devices with their start and end apart: 26, of which 20 were waited for; matrix products, arithmetic and copies ran while one was open for 10% of the time, Pallas kernels for 0%

commit v1 on v0

--- a/solution.py
+++ b/solution.py
@@ -189,7 +189,10 @@
         )
 
     def regroup(values):
-        return lax.all_to_all(values, "col", split_axis=1, concat_axis=1, tiled=True)
+        return jnp.concatenate(
+            lax.all_to_all(jnp.stack(jnp.split(values, lax.axis_size("col"), axis=1)), "col", 0, 0),
+            axis=1,
+        )
 
     def only_mesh(worker, fallback, operands):
         return lax.cond(on_mesh, lambda packed: worker(*packed), lambda packed: fallback, operands)

time: 187 us -> 193 us (1.032)
  blocking collectives: 27.7 us -> 11.2 us
  waiting for transfers between devices: 77.1 us -> 86.4 us
  starting transfers between devices: 50.6 us -> 58.5 us
  local copies, waits for them, and re-layouts: 11.2 us -> 16.5 us
    all_to_all x2 -> x1, blocking collectives: 27.7 us -> 11.2 us  [regroup(): lax.all_to_all(jnp.stack(jnp.split(values, lax.axis_size('col'), axis=1))...]
    all_to_all x1 -> x2, waiting for transfers between devices: 0.01 us -> 8.79 us  [regroup(): lax.all_to_all(jnp.stack(jnp.split(values, lax.axis_size('col'), axis=1))...]
    all_to_all x1 -> x2, starting transfers between devices: 3.54 us -> 11.4 us  [regroup(): lax.all_to_all(jnp.stack(jnp.split(values, lax.axis_size('col'), axis=1))...]
    unnamed x9 -> x30, local copies, waits for them, and re-layouts: 2.94 us -> 7.88 us
  transfers between devices with their start and end apart: 26 -> 27, of which waited for: 20 -> 21; matrix products, arithmetic and copies ran while one was open for 10% -> 9% of each run, Pallas kernels for 0% -> 0%
where the time goes in v1:
time: 193 us
  waiting for transfers between devices  86.4 us (45%)
  starting transfers between devices  58.5 us (30%)
  other arithmetic  18.6 us (10%)
  local copies, waits for them, and re-layouts  16.5 us (9%)
  blocking collectives  11.2 us (6%)
    ppermute x12, waiting for transfers between devices, with_halo(): lax.ppermute(tail, axis, [(i, (i + 1) % count) for i in range(count)])  49 us
    ppermute x12, starting transfers between devices, with_halo(): lax.ppermute(head, axis, [((i + 1) % count, i) for i in range(count)])  27.5 us
    ppermute x12, waiting for transfers between devices, with_halo(): lax.ppermute(head, axis, [((i + 1) % count, i) for i in range(count)])  27 us
    ppermute x12, starting transfers between devices, with_halo(): lax.ppermute(tail, axis, [(i, (i + 1) % count) for i in range(count)])  19.4 us
    all_to_all x2, starting transfers between devices, regroup(): lax.all_to_all(jnp.stack(jnp.split(values, lax.axis_size('col'), axis=1))...  11.4 us
    all_to_all x1, blocking collectives, regroup(): lax.all_to_all(jnp.stack(jnp.split(values, lax.axis_size('col'), axis=1))...  11.2 us
    all_to_all x2, waiting for transfers between devices, regroup(): lax.all_to_all(jnp.stack(jnp.split(values, lax.axis_size('col'), axis=1))...  8.79 us
    unnamed x30, local copies, waits for them, and re-layouts  7.88 us
  transfers between devices with their start and end apart: 27, of which 21 were waited for; matrix products, arithmetic and copies ran while one was open for 9% of the time, Pallas kernels for 0%

profile of v1, /device:TPU:0, one launch (start us, length us, event | category | flops | bytes accessed | tf_op | source)
XLA Modules:
  0.0 193.0 jit_solution(1690122038663552899)
XLA Ops:
  0.0 0.9 copy.208
  1.0 1.1 slice_bitcast_fusion.9
  7.1 7.9 %all-to-all-start = ((f32[8,2,1,8,512]{4,3,1,2,0:T(8,128)}), f32[8,2,1,8,512]{4,3,1,2,0:T(8,128)S(1)}, u32[]{:S(2)}, u32[]{:S(2)}) async-start(f32[8,2,1,8,512]{4,3,1,2,0:T(8,128)} %constant_dynamic-update-slice_fusion.12), calls=%async_computation | async-start | bytes 524288 | tf_op jit(solution)/shard_map/all_to_all | solution.py:193
  15.0 8.8 %all-to-all-done = f32[8,2,1,8,512]{4,3,1,2,0:T(8,128)S(1)} async-done(((f32[8,2,1,8,512]{4,3,1,2,0:T(8,128)}), f32[8,2,1,8,512]{4,3,1,2,0:T(8,128)S(1)}, u32[]{:S(2)}, u32[]{:S(2)}) %all-to-all-start) | async-done | bytes 262176 | tf_op jit(solution)/shard_map/all_to_all | solution.py:193
  23.9 3.7 %collective-permute-start.1 = (f32[4,2,4096]{2,1,0:T(2,128)S(1)}, f32[4,2,4096]{2,1,0:T(2,128)S(1)}, u32[]{:S(2)}, u32[]{:S(2)}) collective-permute-start(f32[4,2,4096]{2,1,0:T(2,128)S(1)} %get-tuple-element.352), channel_id=1, source_target_pairs={{1,0},{2,1},{3,2},{4,3},{5,4},{6,5},{7,6},{8,7},{9,8},{10,9},{11,1... | collective-permute-start | bytes 393224 | tf_op jit(solution)/shard_map/ppermute | solution.py:34
  27.7 3.0 %collective-permute-start.9 = (f32[7,2,512]{2,1,0:T(2,128)S(1)}, f32[7,2,512]{2,1,0:T(2,128)S(1)}, u32[]{:S(2)}, u32[]{:S(2)}) collective-permute-start(f32[7,2,512]{2,1,0:T(2,128)S(1)} %get-tuple-element.330), channel_id=1, source_target_pairs={{8,0},{16,8},{24,16},{32,24},{40,32},{48,40},{56,48},{0,56},{9,1},... | collective-permute-start | bytes 86024 | tf_op jit(solution)/shard_map/ppermute | solution.py:34
  30.7 0.9 collective-permute-done.1
  31.6 6.7 %collective-permute-done = f32[4,2,4096]{2,1,0:T(2,128)S(1)} collective-permute-done((f32[4,2,4096]{2,1,0:T(2,128)S(1)}, f32[4,2,4096]{2,1,0:T(2,128)S(1)}, u32[]{:S(2)}, u32[]{:S(2)}) %collective-permute-start) | collective-permute-done | bytes 131104 | tf_op jit(solution)/shard_map/ppermute | solution.py:32
  38.6 0.9 copy-done.1
  39.5 1.6 concatenate.79
  41.2 1.3 collective-permute-start.3
  42.6 2.3 %collective-permute-start.2 = (f32[2,1,4096]{2,1,0:T(1,128)S(1)}, f32[2,1,4096]{2,1,0:T(1,128)S(1)}, u32[]{:S(2)}, u32[]{:S(2)}) collective-permute-start(f32[2,1,4096]{2,1,0:T(1,128)S(1)} %get-tuple-element.363), channel_id=1, source_target_pairs={{0,1},{1,2},{2,3},{3,4},{4,5},{5,6},{6,7},{7,8},{8,9},{9,10},{10,1... | collective-permute-start | bytes 98312 | tf_op jit(solution)/shard_map/ppermute | solution.py:32
  45.0 1.4 collective-permute-start.11
  46.5 2.2 %collective-permute-start.10 = (f32[7,68,2]{2,1,0:T(8,128)S(1)}, f32[7,68,2]{2,1,0:T(8,128)}, u32[]{:S(2)}, u32[]{:S(2)}) collective-permute-start(f32[7,68,2]{2,1,0:T(8,128)S(1)} %get-tuple-element.325), channel_id=1, source_target_pairs={{0,1},{1,2},{2,3},{3,4},{4,5},{5,6},{6,7},{7,0},{8,9},{9,10},{10,1... | collective-permute-start | bytes 11432 | tf_op jit(solution)/shard_map/ppermute | solution.py:32
  48.6 7.2 %collective-permute-done.3 = f32[2,1,4096]{2,1,0:T(1,128)S(1)} collective-permute-done((f32[2,1,4096]{2,1,0:T(1,128)S(1)}, f32[2,1,4096]{2,1,0:T(1,128)S(1)}, u32[]{:S(2)}, u32[]{:S(2)}) %collective-permute-start.3) | collective-permute-done | bytes 32800 | tf_op jit(solution)/shard_map/ppermute | solution.py:34
  55.8 3.7 %collective-permute-done.2 = f32[2,1,4096]{2,1,0:T(1,128)S(1)} collective-permute-done((f32[2,1,4096]{2,1,0:T(1,128)S(1)}, f32[2,1,4096]{2,1,0:T(1,128)S(1)}, u32[]{:S(2)}, u32[]{:S(2)}) %collective-permute-start.2) | collective-permute-done | bytes 32800 | tf_op jit(solution)/shard_map/ppermute | solution.py:32
  60.0 4.3 %collective-permute-start.5 = (f32[2,1,4096]{2,1,0:T(1,128)S(1)}, f32[2,1,4096]{2,1,0:T(1,128)S(1)}, u32[]{:S(2)}, u32[]{:S(2)}) collective-permute-start(f32[2,1,4096]{2,1,0:T(1,128)S(1)} %get-tuple-element.362), channel_id=1, source_target_pairs={{1,0},{2,1},{3,2},{4,3},{5,4},{6,5},{7,6},{8,7},{9,8},{10,9},{11,1... | collective-permute-start | bytes 98312 | tf_op jit(solution)/shard_map/ppermute | solution.py:34
  64.3 1.7 pad_maximum_fusion
  66.0 6.8 %conditional.17 = (f32[5,64,512]{2,1,0:T(8,128)S(1)}) conditional(s32[]{:T(128)} %convert_element_type.2, (f32[7,68,516]{2,1,0:T(8,128)S(1)}, f32[5,64,512]{2,1,0:T(8,128)S(1)}) %tuple.239, f32[5,64,512]{2,1,0:T(8,128)S(1)} %copy-done), branch_computations={%region_10.11_spmd, %region_11.12_spmd} | conditional | flops 12940432 | bytes 60802312 | solution.py:221
  74.1 6.7 %collective-permute-start.7 = (f32[2,1,4096]{2,1,0:T(1,128)S(1)}, f32[2,1,4096]{2,1,0:T(1,128)S(1)}, u32[]{:S(2)}, u32[]{:S(2)}) collective-permute-start(f32[2,1,4096]{2,1,0:T(1,128)S(1)} %get-tuple-element.360), channel_id=1, source_target_pairs={{1,0},{2,1},{3,2},{4,3},{5,4},{6,5},{7,6},{8,7},{9,8},{10,9},{11,1... | collective-permute-start | bytes 98312 | tf_op jit(solution)/shard_map/ppermute | solution.py:34
  80.9 1.5 collective-permute-done.7
  82.4 8.2 %collective-permute-done.6 = f32[2,1,4096]{2,1,0:T(1,128)S(1)} collective-permute-done((f32[2,1,4096]{2,1,0:T(1,128)S(1)}, f32[2,1,4096]{2,1,0:T(1,128)S(1)}, u32[]{:S(2)}, u32[]{:S(2)}) %collective-permute-start.6) | collective-permute-done | bytes 32800 | tf_op jit(solution)/shard_map/ppermute | solution.py:32
  91.2 11.2 %all_to_all.15 = f32[8,2,1,8,512]{4,3,1,2,0:T(8,128)S(1)} all-to-all(f32[8,2,1,8,512]{4,3,1,2,0:T(8,128)S(1)} %constant_dynamic-update-slice_fusion.22), channel_id=1, replica_groups=mesh['grp'=2,'row'=8,'col'=8] {'col'}, dimensions={0} | all-to-all | bytes 524288 | tf_op jit(solution)/shard_map/all_to_all | solution.py:193
  102.5 1.5 collective-permute-done.12
  104.1 1.2 collective-permute-start.14
  105.3 2.4 %collective-permute-start.13 = (f32[4,2,4096]{2,1,0:T(2,128)S(1)}, f32[4,2,4096]{2,1,0:T(2,128)S(1)}, u32[]{:S(2)}, u32[]{:S(2)}) collective-permute-start(f32[4,2,4096]{2,1,0:T(2,128)S(1)} %get-tuple-element.343), channel_id=1, source_target_pairs={{0,1},{1,2},{2,3},{3,4},{4,5},{5,6},{6,7},{7,8},{8,9},{9,10},{10,1... | collective-permute-start | bytes 393224 | tf_op jit(solution)/shard_map/ppermute | solution.py:32
  107.7 4.3 %collective-permute-done.14 = f32[4,2,4096]{2,1,0:T(2,128)S(1)} collective-permute-done((f32[4,2,4096]{2,1,0:T(2,128)S(1)}, f32[4,2,4096]{2,1,0:T(2,128)S(1)}, u32[]{:S(2)}, u32[]{:S(2)}) %collective-permute-start.14) | collective-permute-done | bytes 131104 | tf_op jit(solution)/shard_map/ppermute | solution.py:34
  112.0 4.3 %collective-permute-done.13 = f32[4,2,4096]{2,1,0:T(2,128)S(1)} collective-permute-done((f32[4,2,4096]{2,1,0:T(2,128)S(1)}, f32[4,2,4096]{2,1,0:T(2,128)S(1)}, u32[]{:S(2)}, u32[]{:S(2)}) %collective-permute-start.13) | collective-permute-done | bytes 131104 | tf_op jit(solution)/shard_map/ppermute | solution.py:32
  116.6 0.9 copy-done.2
  117.5 1.7 concatenate.91
  120.4 3.5 %collective-permute-start.15 = (f32[2,1,4096]{2,1,0:T(1,128)S(1)}, f32[2,1,4096]{2,1,0:T(1,128)S(1)}, u32[]{:S(2)}, u32[]{:S(2)}) collective-permute-start(f32[2,1,4096]{2,1,0:T(1,128)S(1)} %get-tuple-element.357), channel_id=1, source_target_pairs={{0,1},{1,2},{2,3},{3,4},{4,5},{5,6},{6,7},{7,8},{8,9},{9,10},{10,1... | collective-permute-start | bytes 98312 | tf_op jit(solution)/shard_map/ppermute | solution.py:32
  123.9 1.9 collective-permute-done.16
  125.8 4.0 %collective-permute-done.15 = f32[2,1,4096]{2,1,0:T(1,128)S(1)} collective-permute-done((f32[2,1,4096]{2,1,0:T(1,128)S(1)}, f32[2,1,4096]{2,1,0:T(1,128)S(1)}, u32[]{:S(2)}, u32[]{:S(2)}) %collective-permute-start.15) | collective-permute-done | bytes 32800 | tf_op jit(solution)/shard_map/ppermute | solution.py:32
  130.4 3.5 %collective-permute-start.17 = (f32[2,1,4096]{2,1,0:T(1,128)S(1)}, f32[2,1,4096]{2,1,0:T(1,128)S(1)}, u32[]{:S(2)}, u32[]{:S(2)}) collective-permute-start(f32[2,1,4096]{2,1,0:T(1,128)S(1)} %get-tuple-element.355), channel_id=1, source_target_pairs={{0,1},{1,2},{2,3},{3,4},{4,5},{5,6},{6,7},{7,8},{8,9},{9,10},{10,1... | collective-permute-start | bytes 98312 | tf_op jit(solution)/shard_map/ppermute | solution.py:32
  133.9 1.9 collective-permute-done.18
  135.8 4.0 %collective-permute-done.17 = f32[2,1,4096]{2,1,0:T(1,128)S(1)} collective-permute-done((f32[2,1,4096]{2,1,0:T(1,128)S(1)}, f32[2,1,4096]{2,1,0:T(1,128)S(1)}, u32[]{:S(2)}, u32[]{:S(2)}) %collective-permute-start.17) | collective-permute-done | bytes 32800 | tf_op jit(solution)/shard_map/ppermute | solution.py:32
  140.5 3.5 %collective-permute-start.19 = (f32[2,1,4096]{2,1,0:T(1,128)S(1)}, f32[2,1,4096]{2,1,0:T(1,128)S(1)}, u32[]{:S(2)}, u32[]{:S(2)}) collective-permute-start(f32[2,1,4096]{2,1,0:T(1,128)S(1)} %get-tuple-element.353), channel_id=1, source_target_pairs={{0,1},{1,2},{2,3},{3,4},{4,5},{5,6},{6,7},{7,8},{8,9},{9,10},{10,1... | collective-permute-start | bytes 98312 | tf_op jit(solution)/shard_map/ppermute | solution.py:32
  144.0 1.9 collective-permute-done.20
  145.9 7.6 %collective-permute-done.19 = f32[2,1,4096]{2,1,0:T(1,128)S(1)} collective-permute-done((f32[2,1,4096]{2,1,0:T(1,128)S(1)}, f32[2,1,4096]{2,1,0:T(1,128)S(1)}, u32[]{:S(2)}, u32[]{:S(2)}) %collective-permute-start.19) | collective-permute-done | bytes 32800 | tf_op jit(solution)/shard_map/ppermute | solution.py:32
  156.0 3.5 %all-to-all-start.2 = ((f32[8,5,1,8,512]{4,3,1,2,0:T(8,128)}), f32[8,5,1,8,512]{4,3,1,2,0:T(8,128)S(1)}, u32[]{:S(2)}, u32[]{:S(2)}) async-start(f32[8,5,1,8,512]{4,3,1,2,0:T(8,128)} %copy.57), calls=%async_computation.2 | async-start | bytes 1310720 | tf_op jit(solution)/shard_map/all_to_all | solution.py:193
  159.6 2.0 %collective-permute-start.21 = (f32[7,2,512]{2,1,0:T(2,128)S(1)}, f32[7,2,512]{2,1,0:T(2,128)S(1)}, u32[]{:S(2)}, u32[]{:S(2)}) collective-permute-start(f32[7,2,512]{2,1,0:T(2,128)S(1)} %get-tuple-element.327), channel_id=1, source_target_pairs={{0,8},{8,16},{16,24},{24,32},{32,40},{40,48},{48,56},{56,0},{1,9},... | collective-permute-start | bytes 86024 | tf_op jit(solution)/shard_map/ppermute | solution.py:32
  161.7 2.9 %collective-permute-done.22 = f32[7,2,512]{2,1,0:T(2,128)S(1)} collective-permute-done((f32[7,2,512]{2,1,0:T(2,128)S(1)}, f32[7,2,512]{2,1,0:T(2,128)S(1)}, u32[]{:S(2)}, u32[]{:S(2)}) %collective-permute-start.22) | collective-permute-done | bytes 28704 | tf_op jit(solution)/shard_map/ppermute | solution.py:34
  164.6 1.4 collective-permute-done.21
  166.2 5.6 %collective-permute-start.24 = (f32[7,68,2]{2,1,0:T(8,128)S(1)}, f32[7,68,2]{2,1,0:T(8,128)S(1)}, u32[]{:S(2)}, u32[]{:S(2)}) collective-permute-start(f32[7,68,2]{2,1,0:T(8,128)S(1)} %get-tuple-element.324), channel_id=1, source_target_pairs={{1,0},{2,1},{3,2},{4,3},{5,4},{6,5},{7,6},{0,7},{9,8},{10,9},{11,1... | collective-permute-start | bytes 11432 | tf_op jit(solution)/shard_map/ppermute | solution.py:34
  171.8 4.4 %collective-permute-done.24 = f32[7,68,2]{2,1,0:T(8,128)S(1)} collective-permute-done((f32[7,68,2]{2,1,0:T(8,128)S(1)}, f32[7,68,2]{2,1,0:T(8,128)S(1)}, u32[]{:S(2)}, u32[]{:S(2)}) %collective-permute-start.24) | collective-permute-done | bytes 3840 | tf_op jit(solution)/shard_map/ppermute | solution.py:34
  176.2 8.3 %collective-permute-done.23 = f32[7,68,2]{2,1,0:T(8,128)S(1)} collective-permute-done((f32[7,68,2]{2,1,0:T(8,128)S(1)}, f32[7,68,2]{2,1,0:T(8,128)S(1)}, u32[]{:S(2)}, u32[]{:S(2)}) %collective-permute-start.23) | collective-permute-done | bytes 3840 | tf_op jit(solution)/shard_map/ppermute | solution.py:32
  185.1 6.9 %conditional.23 = (f32[5,64,512]{2,1,0:T(8,128)S(1)}) conditional(s32[]{:T(128)} %convert_element_type.2, (f32[7,68,516]{2,1,0:T(8,128)S(1)}, f32[5,64,512]{2,1,0:T(8,128)S(1)}) %tuple.90, f32[5,64,512]{2,1,0:T(8,128)S(1)} %get-tuple-element.376), branch_computations={%region_22.23_spmd, %region_23.24_spmd} | conditional | flops 12940432 | bytes 60802312 | solution.py:221
  192.0 0.9 fusion.218
  (199 shorter events, 27.6 us)
Async XLA Ops:
  7.1 16.7 %all-to-all-start = ((f32[8,2,1,8,512]{4,3,1,2,0:T(8,128)}), f32[8,2,1,8,512]{4,3,1,2,0:T(8,128)S(1)}, u32[]{:S(2)}, u32[]{:S(2)}) async-start(f32[8,2,1,8,512]{4,3,1,2,0:T(8,128)} %constant_dynamic-update-slice_fusion.12), calls=%async_computation | async-start | bytes 524288 | tf_op jit(solution)/shard_map/all_to_all | solution.py:193
  23.8 3.9 %copy-start = (f32[5,64,512]{2,1,0:T(8,128)S(1)}, f32[5,64,512]{2,1,0:T(8,128)}, u32[]{:S(2)}) copy-start(f32[5,64,512]{2,1,0:T(8,128)} %param.26) | copy-start | bytes 1966084
  23.9 7.7 %collective-permute-start.1 = (f32[4,2,4096]{2,1,0:T(2,128)S(1)}, f32[4,2,4096]{2,1,0:T(2,128)S(1)}, u32[]{:S(2)}, u32[]{:S(2)}) collective-permute-start(f32[4,2,4096]{2,1,0:T(2,128)S(1)} %get-tuple-element.352), channel_id=1, source_target_pairs={{1,0},{2,1},{3,2},{4,3},{5,4},{6,5},{7,6},{8,7},{9,8},{10,9},{11,1... | collective-permute-start | bytes 393224 | tf_op jit(solution)/shard_map/ppermute | solution.py:34
  27.6 10.7 %collective-permute-start = (f32[4,2,4096]{2,1,0:T(2,128)S(1)}, f32[4,2,4096]{2,1,0:T(2,128)S(1)}, u32[]{:S(2)}, u32[]{:S(2)}) collective-permute-start(f32[4,2,4096]{2,1,0:T(2,128)S(1)} %get-tuple-element.351), channel_id=1, source_target_pairs={{0,1},{1,2},{2,3},{3,4},{4,5},{5,6},{6,7},{7,8},{8,9},{9,10},{10,1... | collective-permute-start | bytes 393224 | tf_op jit(solution)/shard_map/ppermute | solution.py:32
  27.7 17.1 %collective-permute-start.9 = (f32[7,2,512]{2,1,0:T(2,128)S(1)}, f32[7,2,512]{2,1,0:T(2,128)S(1)}, u32[]{:S(2)}, u32[]{:S(2)}) collective-permute-start(f32[7,2,512]{2,1,0:T(2,128)S(1)} %get-tuple-element.330), channel_id=1, source_target_pairs={{8,0},{16,8},{24,16},{32,24},{40,32},{48,40},{56,48},{0,56},{9,1},... | collective-permute-start | bytes 86024 | tf_op jit(solution)/shard_map/ppermute | solution.py:34
  30.7 14.1 %collective-permute-start.8 = (f32[7,2,512]{2,1,0:T(2,128)S(1)}, f32[7,2,512]{2,1,0:T(2,128)S(1)}, u32[]{:S(2)}, u32[]{:S(2)}) collective-permute-start(f32[7,2,512]{2,1,0:T(2,128)S(1)} %get-tuple-element.329), channel_id=1, source_target_pairs={{0,8},{8,16},{16,24},{24,32},{32,40},{40,48},{48,56},{56,0},{1,9},... | collective-permute-start | bytes 86024 | tf_op jit(solution)/shard_map/ppermute | solution.py:32
  38.5 1.0 copy-start.1
  41.2 14.6 %collective-permute-start.3 = (f32[2,1,4096]{2,1,0:T(1,128)S(1)}, f32[2,1,4096]{2,1,0:T(1,128)S(1)}, u32[]{:S(2)}, u32[]{:S(2)}) collective-permute-start(f32[2,1,4096]{2,1,0:T(1,128)S(1)} %get-tuple-element.364), channel_id=1, source_target_pairs={{1,0},{2,1},{3,2},{4,3},{5,4},{6,5},{7,6},{8,7},{9,8},{10,9},{11,1... | collective-permute-start | bytes 98312 | tf_op jit(solution)/shard_map/ppermute | solution.py:34
  42.6 17.0 %collective-permute-start.2 = (f32[2,1,4096]{2,1,0:T(1,128)S(1)}, f32[2,1,4096]{2,1,0:T(1,128)S(1)}, u32[]{:S(2)}, u32[]{:S(2)}) collective-permute-start(f32[2,1,4096]{2,1,0:T(1,128)S(1)} %get-tuple-element.363), channel_id=1, source_target_pairs={{0,1},{1,2},{2,3},{3,4},{4,5},{5,6},{6,7},{7,8},{8,9},{9,10},{10,1... | collective-permute-start | bytes 98312 | tf_op jit(solution)/shard_map/ppermute | solution.py:32
  45.0 19.3 %collective-permute-start.11 = (f32[7,68,2]{2,1,0:T(8,128)S(1)}, f32[7,68,2]{2,1,0:T(8,128)}, u32[]{:S(2)}, u32[]{:S(2)}) collective-permute-start(f32[7,68,2]{2,1,0:T(8,128)S(1)} %get-tuple-element.326), channel_id=1, source_target_pairs={{1,0},{2,1},{3,2},{4,3},{5,4},{6,5},{7,6},{0,7},{9,8},{10,9},{11,1... | collective-permute-start | bytes 11432 | tf_op jit(solution)/shard_map/ppermute | solution.py:34
  46.5 17.9 %collective-permute-start.10 = (f32[7,68,2]{2,1,0:T(8,128)S(1)}, f32[7,68,2]{2,1,0:T(8,128)}, u32[]{:S(2)}, u32[]{:S(2)}) collective-permute-start(f32[7,68,2]{2,1,0:T(8,128)S(1)} %get-tuple-element.325), channel_id=1, source_target_pairs={{0,1},{1,2},{2,3},{3,4},{4,5},{5,6},{6,7},{7,0},{8,9},{9,10},{10,1... | collective-permute-start | bytes 11432 | tf_op jit(solution)/shard_map/ppermute | solution.py:32
  60.0 12.7 %collective-permute-start.5 = (f32[2,1,4096]{2,1,0:T(1,128)S(1)}, f32[2,1,4096]{2,1,0:T(1,128)S(1)}, u32[]{:S(2)}, u32[]{:S(2)}) collective-permute-start(f32[2,1,4096]{2,1,0:T(1,128)S(1)} %get-tuple-element.362), channel_id=1, source_target_pairs={{1,0},{2,1},{3,2},{4,3},{5,4},{6,5},{7,6},{8,7},{9,8},{10,9},{11,1... | collective-permute-start | bytes 98312 | tf_op jit(solution)/shard_map/ppermute | solution.py:34
  64.3 9.3 %collective-permute-start.4 = (f32[2,1,4096]{2,1,0:T(1,128)S(1)}, f32[2,1,4096]{2,1,0:T(1,128)S(1)}, u32[]{:S(2)}, u32[]{:S(2)}) collective-permute-start(f32[2,1,4096]{2,1,0:T(1,128)S(1)} %get-tuple-element.361), channel_id=1, source_target_pairs={{0,1},{1,2},{2,3},{3,4},{4,5},{5,6},{6,7},{7,8},{8,9},{9,10},{10,1... | collective-permute-start | bytes 98312 | tf_op jit(solution)/shard_map/ppermute | solution.py:32
  74.1 8.3 %collective-permute-start.7 = (f32[2,1,4096]{2,1,0:T(1,128)S(1)}, f32[2,1,4096]{2,1,0:T(1,128)S(1)}, u32[]{:S(2)}, u32[]{:S(2)}) collective-permute-start(f32[2,1,4096]{2,1,0:T(1,128)S(1)} %get-tuple-element.360), channel_id=1, source_target_pairs={{1,0},{2,1},{3,2},{4,3},{5,4},{6,5},{7,6},{8,7},{9,8},{10,9},{11,1... | collective-permute-start | bytes 98312 | tf_op jit(solution)/shard_map/ppermute | solution.py:34
  80.8 9.8 %collective-permute-start.6 = (f32[2,1,4096]{2,1,0:T(1,128)S(1)}, f32[2,1,4096]{2,1,0:T(1,128)S(1)}, u32[]{:S(2)}, u32[]{:S(2)}) collective-permute-start(f32[2,1,4096]{2,1,0:T(1,128)S(1)} %get-tuple-element.359), channel_id=1, source_target_pairs={{0,1},{1,2},{2,3},{3,4},{4,5},{5,6},{6,7},{7,8},{8,9},{9,10},{10,1... | collective-permute-start | bytes 98312 | tf_op jit(solution)/shard_map/ppermute | solution.py:32
  102.4 1.6 collective-permute-start.12
  104.1 7.9 %collective-permute-start.14 = (f32[4,2,4096]{2,1,0:T(2,128)S(1)}, f32[4,2,4096]{2,1,0:T(2,128)S(1)}, u32[]{:S(2)}, u32[]{:S(2)}) collective-permute-start(f32[4,2,4096]{2,1,0:T(2,128)S(1)} %get-tuple-element.344), channel_id=1, source_target_pairs={{1,0},{2,1},{3,2},{4,3},{5,4},{6,5},{7,6},{8,7},{9,8},{10,9},{11,1... | collective-permute-start | bytes 393224 | tf_op jit(solution)/shard_map/ppermute | solution.py:34
  105.3 11.0 %collective-permute-start.13 = (f32[4,2,4096]{2,1,0:T(2,128)S(1)}, f32[4,2,4096]{2,1,0:T(2,128)S(1)}, u32[]{:S(2)}, u32[]{:S(2)}) collective-permute-start(f32[4,2,4096]{2,1,0:T(2,128)S(1)} %get-tuple-element.343), channel_id=1, source_target_pairs={{0,1},{1,2},{2,3},{3,4},{4,5},{5,6},{6,7},{7,8},{8,9},{9,10},{10,1... | collective-permute-start | bytes 393224 | tf_op jit(solution)/shard_map/ppermute | solution.py:32
  116.5 1.0 copy-start.2
  120.3 5.5 %collective-permute-start.16 = (f32[2,1,4096]{2,1,0:T(1,128)S(1)}, f32[2,1,4096]{2,1,0:T(1,128)S(1)}, u32[]{:S(2)}, u32[]{:S(2)}) collective-permute-start(f32[2,1,4096]{2,1,0:T(1,128)S(1)} %get-tuple-element.358), channel_id=1, source_target_pairs={{1,0},{2,1},{3,2},{4,3},{5,4},{6,5},{7,6},{8,7},{9,8},{10,9},{11,1... | collective-permute-start | bytes 98312 | tf_op jit(solution)/shard_map/ppermute | solution.py:34
  120.4 9.4 %collective-permute-start.15 = (f32[2,1,4096]{2,1,0:T(1,128)S(1)}, f32[2,1,4096]{2,1,0:T(1,128)S(1)}, u32[]{:S(2)}, u32[]{:S(2)}) collective-permute-start(f32[2,1,4096]{2,1,0:T(1,128)S(1)} %get-tuple-element.357), channel_id=1, source_target_pairs={{0,1},{1,2},{2,3},{3,4},{4,5},{5,6},{6,7},{7,8},{8,9},{9,10},{10,1... | collective-permute-start | bytes 98312 | tf_op jit(solution)/shard_map/ppermute | solution.py:32
  130.3 5.5 %collective-permute-start.18 = (f32[2,1,4096]{2,1,0:T(1,128)S(1)}, f32[2,1,4096]{2,1,0:T(1,128)S(1)}, u32[]{:S(2)}, u32[]{:S(2)}) collective-permute-start(f32[2,1,4096]{2,1,0:T(1,128)S(1)} %get-tuple-element.356), channel_id=1, source_target_pairs={{1,0},{2,1},{3,2},{4,3},{5,4},{6,5},{7,6},{8,7},{9,8},{10,9},{11,1... | collective-permute-start | bytes 98312 | tf_op jit(solution)/shard_map/ppermute | solution.py:34
  130.4 9.4 %collective-permute-start.17 = (f32[2,1,4096]{2,1,0:T(1,128)S(1)}, f32[2,1,4096]{2,1,0:T(1,128)S(1)}, u32[]{:S(2)}, u32[]{:S(2)}) collective-permute-start(f32[2,1,4096]{2,1,0:T(1,128)S(1)} %get-tuple-element.355), channel_id=1, source_target_pairs={{0,1},{1,2},{2,3},{3,4},{4,5},{5,6},{6,7},{7,8},{8,9},{9,10},{10,1... | collective-permute-start | bytes 98312 | tf_op jit(solution)/shard_map/ppermute | solution.py:32
  140.4 5.5 %collective-permute-start.20 = (f32[2,1,4096]{2,1,0:T(1,128)S(1)}, f32[2,1,4096]{2,1,0:T(1,128)S(1)}, u32[]{:S(2)}, u32[]{:S(2)}) collective-permute-start(f32[2,1,4096]{2,1,0:T(1,128)S(1)} %get-tuple-element.354), channel_id=1, source_target_pairs={{1,0},{2,1},{3,2},{4,3},{5,4},{6,5},{7,6},{8,7},{9,8},{10,9},{11,1... | collective-permute-start | bytes 98312 | tf_op jit(solution)/shard_map/ppermute | solution.py:34
  140.5 13.0 %collective-permute-start.19 = (f32[2,1,4096]{2,1,0:T(1,128)S(1)}, f32[2,1,4096]{2,1,0:T(1,128)S(1)}, u32[]{:S(2)}, u32[]{:S(2)}) collective-permute-start(f32[2,1,4096]{2,1,0:T(1,128)S(1)} %get-tuple-element.353), channel_id=1, source_target_pairs={{0,1},{1,2},{2,3},{3,4},{4,5},{5,6},{6,7},{7,8},{8,9},{9,10},{10,1... | collective-permute-start | bytes 98312 | tf_op jit(solution)/shard_map/ppermute | solution.py:32
  156.0 36.0 %all-to-all-start.2 = ((f32[8,5,1,8,512]{4,3,1,2,0:T(8,128)}), f32[8,5,1,8,512]{4,3,1,2,0:T(8,128)S(1)}, u32[]{:S(2)}, u32[]{:S(2)}) async-start(f32[8,5,1,8,512]{4,3,1,2,0:T(8,128)} %copy.57), calls=%async_computation.2 | async-start | bytes 1310720 | tf_op jit(solution)/shard_map/all_to_all | solution.py:193
  159.6 5.0 %collective-permute-start.22 = (f32[7,2,512]{2,1,0:T(2,128)S(1)}, f32[7,2,512]{2,1,0:T(2,128)S(1)}, u32[]{:S(2)}, u32[]{:S(2)}) collective-permute-start(f32[7,2,512]{2,1,0:T(2,128)S(1)} %get-tuple-element.328), channel_id=1, source_target_pairs={{8,0},{16,8},{24,16},{32,24},{40,32},{48,40},{56,48},{0,56},{9,1},... | collective-permute-start | bytes 86024 | tf_op jit(solution)/shard_map/ppermute | solution.py:34
  159.6 6.4 %collective-permute-start.21 = (f32[7,2,512]{2,1,0:T(2,128)S(1)}, f32[7,2,512]{2,1,0:T(2,128)S(1)}, u32[]{:S(2)}, u32[]{:S(2)}) collective-permute-start(f32[7,2,512]{2,1,0:T(2,128)S(1)} %get-tuple-element.327), channel_id=1, source_target_pairs={{0,8},{8,16},{16,24},{24,32},{32,40},{40,48},{48,56},{56,0},{1,9},... | collective-permute-start | bytes 86024 | tf_op jit(solution)/shard_map/ppermute | solution.py:32
  166.2 10.0 %collective-permute-start.24 = (f32[7,68,2]{2,1,0:T(8,128)S(1)}, f32[7,68,2]{2,1,0:T(8,128)S(1)}, u32[]{:S(2)}, u32[]{:S(2)}) collective-permute-start(f32[7,68,2]{2,1,0:T(8,128)S(1)} %get-tuple-element.324), channel_id=1, source_target_pairs={{1,0},{2,1},{3,2},{4,3},{5,4},{6,5},{7,6},{0,7},{9,8},{10,9},{11,1... | collective-permute-start | bytes 11432 | tf_op jit(solution)/shard_map/ppermute | solution.py:34
  171.8 12.7 %collective-permute-start.23 = (f32[7,68,2]{2,1,0:T(8,128)S(1)}, f32[7,68,2]{2,1,0:T(8,128)S(1)}, u32[]{:S(2)}, u32[]{:S(2)}) collective-permute-start(f32[7,68,2]{2,1,0:T(8,128)S(1)} %get-tuple-element.323), channel_id=1, source_target_pairs={{0,1},{1,2},{2,3},{3,4},{4,5},{5,6},{6,7},{7,0},{8,9},{9,10},{10,1... | collective-permute-start | bytes 11432 | tf_op jit(solution)/shard_map/ppermute | solution.py:32
